TPU v7x, 256 devices: a whole 4x4x8 slice. The times are simulated.
256 devices in a mesh: row: 32 (over z, y_hi, core), col: 8 (over y_lo, x).
Axes of the slice: x: 4, y: 4 (y_hi: 2, y_lo: 2; y = y_hi * 2 + y_lo), z: 8, core: 2. Of those that a mesh axis runs over, the one named last changes fastest.
Arguments:
- obs_summaries: bfloat16 [16384, 256], P(('row', 'col')), may hold values from -6 to 6
- sim_summaries: bfloat16 [8192, 256], P('row'), may hold values from -6 to 6
- neighbours: int32 [16384, 16], P(('row', 'col')), may hold values from 0 to 8191
- field: bfloat16 [8192, 8192], P('row', 'col'), may hold values from -6 to 6
Outputs:
- posterior: bfloat16 [16384, 8192], P('row', 'col')
Inputs may be any that keep to these rules, and one draw needn't show every extreme that they name: `neighbours`: each entry names a row of sim_summaries.
All inputs are finite; a program needn't handle non-finite values.
Results may differ from a plain program's by a relative error of at most 0.005.
Values may be sent and summed in bfloat16 or wider, within the bound.
A program may use at most 128 MiB of HBM per device.

v0:
```python
import jax
import jax.numpy as jnp
from jax import lax
from jax.sharding import PartitionSpec as P

SHARPNESS = 32.0
EPSILON = 1e-06


def neighbour_widths(obs_rows, index_rows, sims_full, sim_square):
    obs_float = obs_rows.astype(jnp.float32)
    near_rows = jnp.take(sims_full, index_rows, axis=0).astype(jnp.float32)
    inner_prod = jnp.einsum("rd,rkd->rk", obs_float, near_rows)
    obs_square = jnp.sum(obs_float * obs_float, axis=1)
    near_square = jnp.take(sim_square, index_rows, axis=0)
    distance = obs_square[:, None] + near_square - 2.0 * inner_prod
    return jnp.mean(distance, axis=1) + EPSILON


def per_device(obs_summaries, sim_summaries, neighbours, field):
    sims_full = lax.all_gather(sim_summaries, "row", axis=0, tiled=True)
    sim_float = sims_full.astype(jnp.float32)
    sim_square = jnp.sum(sim_float * sim_float, axis=1)
    obs_block = lax.all_gather(obs_summaries, "col", axis=0, tiled=True)
    index_block = lax.all_gather(neighbours, "col", axis=0, tiled=True)
    width = neighbour_widths(obs_block, index_block, sims_full, sim_square)
    obs_float = obs_block.astype(jnp.float32)
    obs_square = jnp.sum(obs_float * obs_float, axis=1)
    cross = lax.dot_general(
        obs_block, sims_full, (((1,), (1,)), ((), ())), preferred_element_type=jnp.float32
    )
    distance = obs_square[:, None] + sim_square[None, :] - 2.0 * cross
    weight = jnp.exp(-SHARPNESS * distance / width[:, None])
    numer = jnp.dot(
        weight.astype(jnp.bfloat16),
        lax.all_gather(field, "row", axis=0, tiled=True),
        preferred_element_type=jnp.float32,
    )
    total = jnp.sum(weight, axis=1)
    numer, total = (numer, total)
    return (numer / total[:, None]).astype(jnp.bfloat16)


def solution(mesh):
    return jax.shard_map(
        per_device,
        mesh=mesh,
        in_specs=(
            P(("row", "col"), None),
            P("row", None),
            P(("row", "col"), None),
            P("row", "col"),
        ),
        out_specs=P("row", "col"),
        check_vma=False,
    )
```

profile of v0, /device:TPU:1, one launch (start us, length us, event | category | flops | bytes accessed | tf_op | source)
XLA Modules:
  0.0 260.9 jit_solution(11695345352077202125)
XLA Ops:
  6.5 0.0 all-gather.4.cloned.1.call-start
  6.5 0.7 all-gather.4.cloned.1.call-update
  7.3 0.0 all-gather.6.cloned.1.call-start
  7.3 0.7 all-gather.6.cloned.1.call-update
  8.0 23.7 %all-gather = s32[8,64,16]{1,2,0:T(8,128)S(1)} all-gather(s32[1,64,16]{1,2,0:T(8,128)} %bitcast.17), channel_id=1, replica_groups=mesh['row'=32,'col'=8] {'col'}, dimensions={0}, use_global_device_ids=true | all-gather | bytes 36864 | tf_op jit(solution)/shard_map/all_gather | solution.py:25
  31.7 0.1 reshape.33
  31.8 0.1 copy.10
  31.9 0.1 reshape.14
  32.1 0.2 copy.12
  32.3 22.7 %all_gather.12 = bf16[512,256]{1,0:T(8,128)(2,1)S(1)} all-gather(bf16[64,256]{1,0:T(8,128)(2,1)} %param.4), channel_id=1, replica_groups=mesh['row'=32,'col'=8] {'col'}, dimensions={0}, use_global_device_ids=true | all-gather | bytes 294912 | tf_op jit(solution)/shard_map/all_gather | solution.py:24
  55.0 0.1 multiply_reduce_fusion.1
  55.2 46.5 %all-gather.4.cloned.1.call-done = bf16[8192,256]{1,0:T(8,128)(2,1)} async-done(((bf16[256,256]{1,0:T(8,128)(2,1)}), bf16[8192,256]{1,0:T(8,128)(2,1)}) %all-gather.4.cloned.1.call-update) | async-done | bytes 4194320 | tf_op jit(solution)/shard_map/all_gather | solution.py:21
  101.7 33.6 %gather_fusion.1 = bf16[8192,256]{1,0:T(8,128)(2,1)} fusion(bf16[8192,256]{1,0:T(8,128)(2,1)} %all-gather.4.cloned.1.call-done, s32[8192]{0:T(1024)S(1)} %broadcast_clamp_fusion), kind=kCustom, calls=%fused_computation.1 | custom fusion | bytes 8421376 | tf_op jit(solution)/shard_map/jit(_take)/gather | solution.py:12
  135.3 5.7 %fusion.2 = f32[512,1,16]{2,1,0:T(1,128)S(1)} fusion(bf16[512,16,256]{2,1,0:T(8,128)(2,1)} %bitcast.15, pred[512,16]{1,0:T(8,128)(4,1)S(1)} %copy.12, bf16[512,256,1]{1,0,2:T(8,128)(2,1)S(1)} %bitcast.16), kind=kOutput, calls=%fused_computation.6 | convolution fusion | flops 6291456 | bytes 4497408 | tf_op jit(solution)/shard_map/rd,rkd->rk/dot_general | solution.py:13
  141.0 0.1 copy.14
  141.1 3.4 %multiply_reduce_fusion = f32[8192]{0:T(1024)S(1)} fusion(bf16[8192,256]{1,0:T(8,128)(2,1)} %all-gather.4.cloned.1.call-done), kind=kLoop, calls=%fused_computation.5 | loop fusion | flops 6283264 | bytes 4227072 | tf_op jit(solution)/shard_map/reduce_sum | solution.py:23
  144.4 45.5 %gather_fusion = f32[8192]{0:T(1024)S(1)} fusion(f32[8192]{0:T(1024)S(1)} %multiply_reduce_fusion, s32[8192]{0:T(1024)S(1)} %broadcast_clamp_fusion), kind=kCustom, calls=%fused_computation | custom fusion | bytes 98304 | tf_op jit(solution)/shard_map/jit(_take)/gather | solution.py:15
  190.0 0.1 reshape.13
  190.1 0.1 copy.11
  190.3 10.0 %fusion.12 = (f32[512]{0:T(512)S(1)}, bf16[512,8192]{1,0:T(8,128)(2,1)}) fusion(f32[512]{0:T(512)S(1)} %multiply_add_fusion, bf16[512,256]{1,0:T(8,128)(2,1)S(1)} %all_gather.12, bf16[8192,256]{1,0:T(8,128)(2,1)} %all-gather.4.cloned.1.call-done, f32[8192]{0:T(1024)S(1)} %multiply_reduce_fusion, f32[512]{0:T(512)S(1)} %multiply_reduce_fusion.1), kind=kOutput, calls=%fused_computation.21 | convolution fusion | flops 2176843264 | bytes 12883968 | tf_op jit(solution)/shard_map/dot_general | solution.py:29
  200.2 38.2 %all-gather.6.cloned.1.call-done = bf16[8192,1024]{1,0:T(8,128)(2,1)} async-done(((bf16[256,1024]{1,0:T(8,128)(2,1)}), bf16[8192,1024]{1,0:T(8,128)(2,1)}) %all-gather.6.cloned.1.call-update) | async-done | bytes 16777232 | tf_op jit(solution)/shard_map/all_gather | solution.py:36
  238.5 15.6 %divide_convert_fusion = bf16[512,1024]{1,0:T(8,128)(2,1)} fusion(bf16[8192,1024]{1,0:T(8,128)(2,1)} %all-gather.6.cloned.1.call-done, bf16[512,8192]{1,0:T(8,128)(2,1)} %get-tuple-element.6, f32[512]{0:T(512)S(1)} %get-tuple-element.5), kind=kOutput, calls=%fused_computation.9 | convolution fusion | flops 8590983168 | bytes 26216448 | tf_op jit(solution)/shard_map/dot_general | solution.py:34
  (6 shorter events, 0.1 us)
Async XLA Ops:
  6.5 95.2 %all-gather.4.cloned.1.call-start = ((), (), s32[]{:S(2)}) async-start(), calls=%async_computation | async-start | bytes 4325376 | tf_op jit(solution)/shard_map/all_gather | solution.py:21
  7.3 231.2 %all-gather.6.cloned.1.call-start = ((), (), s32[]{:S(2)}) async-start(), calls=%async_computation.1 | async-start | bytes 17301504 | tf_op jit(solution)/shard_map/all_gather | solution.py:36
Sparse Core Ops, SparseCore 0:
  10.1 91.5 all-gather.3
  104.5 133.9 all-gather.5
where the time goes:
time: 261 us
  waiting for transfers between devices  86.2 us (33%)
  local copies, waits for them, and re-layouts  80 us (31%)
  blocking collectives  46.4 us (18%)
  matrix products  31.2 us (12%)
  between operations  13.5 us (5%)
  other arithmetic  3.58 us (1%)
    all_gather x1, waiting for transfers between devices, per_device(): sims_full = lax.all_gather(sim_summaries, 'row', axis=0, tiled=True)  46.5 us
    gather x3, local copies, waits for them, and re-layouts, neighbour_widths(): near_square = jnp.take(sim_square, index_rows, axis=0)  45.8 us
    all_gather x1, waiting for transfers between devices, per_device(): lax.all_gather(field, 'row', axis=0, tiled=True)  38.2 us
    gather x1, local copies, waits for them, and re-layouts, neighbour_widths(): near_rows = jnp.take(sims_full, index_rows, axis=0).astype(jnp.float32)  33.6 us
    all_gather x1, blocking collectives, per_device(): index_block = lax.all_gather(neighbours, 'col', axis=0, tiled=True)  23.7 us
    all_gather x1, blocking collectives, per_device(): obs_block = lax.all_gather(obs_summaries, 'col', axis=0, tiled=True)  22.7 us
    dot_general x1, matrix products, per_device(): jnp.dot(weight.astype(jnp.bfloat16), lax.all_gather(field, 'row', axis=0,...  15.6 us
    dot_general x1, matrix products, per_device(): lax.dot_general(obs_block, sims_full, (((1,), (1,)), ((), ())), preferred...  9.97 us
  transfers between devices with their start and end apart: 2, of which 2 were waited for; matrix products, arithmetic and copies ran while one was open for 38% of the time, Pallas kernels for 0%

commit v1 on v0

--- a/solution.py
+++ b/solution.py
@@ -33,7 +33,9 @@
     weight = jnp.exp(-SHARPNESS * distance / width[:, None])
     numer = jnp.dot(
         weight.astype(jnp.bfloat16),
-        lax.all_gather(field, "row", axis=0, tiled=True),
+        jnp.concatenate(
+            lax.all_to_all(jnp.stack([field] * lax.axis_size("row")), "row", 0, 0), axis=0
+        ),
         preferred_element_type=jnp.float32,
     )
     total = jnp.sum(weight, axis=1)

time: 261 us -> 429 us (1.64); the launches traced: 261 us -> 422 us
  waiting for transfers between devices: 86.2 us -> 226 us
  starting transfers between devices: 0.04 us -> 13 us
  local copies, waits for them, and re-layouts: 80 us -> 86.8 us
    all_to_all x0 -> x1, waiting for transfers between devices: none -> 145 us  [per_device(): lax.all_to_all(jnp.stack([field] * lax.axis_size('row')), 'row', 0, 0)]
    all_gather x1 -> x0, waiting for transfers between devices: 38.2 us -> none  [per_device(): lax.all_gather(field, 'row', axis=0, tiled=True)]
    all_gather x1, waiting for transfers between devices: 46.5 us -> 80 us  [per_device(): sims_full = lax.all_gather(sim_summaries, 'row', axis=0, tiled=True)]
    all_to_all x0 -> x1, starting transfers between devices: none -> 12.9 us  [per_device(): lax.all_to_all(jnp.stack([field] * lax.axis_size('row')), 'row', 0, 0)]
    another operation x0 -> x1, local copies, waits for them, and re-layouts: none -> 6.79 us  [per_device(): jnp.stack([field] * lax.axis_size('row'))]
  transfers between devices with their start and end apart: 2 -> 2, of which waited for: 2 -> 2; matrix products, arithmetic and copies ran while one was open for 38% -> 23% of each run, Pallas kernels for 0% -> 0%
where the time goes in v1:
time: 429 us; the launch traced here: 422 us
  waiting for transfers between devices  226 us (53%)
  local copies, waits for them, and re-layouts  86.8 us (20%)
  blocking collectives  48.5 us (11%)
  matrix products  31.1 us (7%)
  between operations  13.5 us (3%)
  starting transfers between devices  13 us (3%)
    all_to_all x1, waiting for transfers between devices, per_device(): lax.all_to_all(jnp.stack([field] * lax.axis_size('row')), 'row', 0, 0)  145 us
    all_gather x1, waiting for transfers between devices, per_device(): sims_full = lax.all_gather(sim_summaries, 'row', axis=0, tiled=True)  80 us
    gather x3, local copies, waits for them, and re-layouts, neighbour_widths(): near_square = jnp.take(sim_square, index_rows, axis=0)  45.8 us
    gather x1, local copies, waits for them, and re-layouts, neighbour_widths(): near_rows = jnp.take(sims_full, index_rows, axis=0).astype(jnp.float32)  33.6 us
    all_gather x1, blocking collectives, per_device(): index_block = lax.all_gather(neighbours, 'col', axis=0, tiled=True)  24.5 us
    all_gather x1, blocking collectives, per_device(): obs_block = lax.all_gather(obs_summaries, 'col', axis=0, tiled=True)  24.1 us
    dot_general x1, matrix products, per_device(): jnp.dot(weight.astype(jnp.bfloat16), jnp.concatenate(lax.all_to_all(jnp.s...  15.6 us
    all_to_all x1, starting transfers between devices, per_device(): lax.all_to_all(jnp.stack([field] * lax.axis_size('row')), 'row', 0, 0)  12.9 us
  transfers between devices with their start and end apart: 2, of which 2 were waited for; matrix products, arithmetic and copies ran while one was open for 23% of the time, Pallas kernels for 0%

profile of v1, /device:TPU:1, one launch (start us, length us, event | category | flops | bytes accessed | tf_op | source)
XLA Modules:
  0.0 422.3 jit_solution(12646992926015121760)
XLA Ops:
  6.5 6.8 %stack.2 = bf16[32,256,1024]{2,1,0:T(8,128)(2,1)} broadcast(bf16[256,1024]{1,0:T(8,128)(2,1)} %param.7), dimensions={1,2} | broadcast | bytes 17301504 | tf_op jit(solution)/shard_map/stack | solution.py:37
  13.3 0.0 copy-start.1
  13.3 0.0 copy-start
  13.3 12.9 %all-to-all-start = ((bf16[32,256,1024]{2,1,0:T(8,128)(2,1)}), bf16[32,256,1024]{2,1,0:T(8,128)(2,1)}, u32[]{:S(2)}, u32[]{:S(2)}) async-start(bf16[32,256,1024]{2,1,0:T(8,128)(2,1)} %stack.2), calls=%async_computation | async-start | bytes 33554432 | tf_op jit(solution)/shard_map/all_to_all | solution.py:37
  26.3 0.0 all-gather.3.cloned.1.call-start
  26.3 0.7 all-gather.3.cloned.1.call-update
  27.0 0.0 copy-done.1
  27.0 24.5 %all-gather = s32[8,64,16]{1,2,0:T(8,128)S(1)} all-gather(s32[1,64,16]{1,2,0:T(8,128)S(1)} %bitcast.18), channel_id=1, replica_groups=mesh['row'=32,'col'=8] {'col'}, dimensions={0}, use_global_device_ids=true | all-gather | bytes 36864 | tf_op jit(solution)/shard_map/all_gather | solution.py:25
  51.5 0.1 reshape.39
  51.6 0.1 copy.10
  51.7 0.1 reshape.20
  51.9 0.2 copy.12
  52.1 0.0 copy-done
  52.1 24.1 %all_gather.9 = bf16[512,256]{1,0:T(8,128)(2,1)S(1)} all-gather(bf16[64,256]{1,0:T(8,128)(2,1)S(1)} %copy-done), channel_id=1, replica_groups=mesh['row'=32,'col'=8] {'col'}, dimensions={0}, use_global_device_ids=true | all-gather | bytes 294912 | tf_op jit(solution)/shard_map/all_gather | solution.py:24
  76.2 0.1 multiply_reduce_fusion.1
  76.3 80.0 %all-gather.3.cloned.1.call-done = bf16[8192,256]{1,0:T(8,128)(2,1)} async-done(((bf16[256,256]{1,0:T(8,128)(2,1)}), bf16[8192,256]{1,0:T(8,128)(2,1)}) %all-gather.3.cloned.1.call-update) | async-done | bytes 4194320 | tf_op jit(solution)/shard_map/all_gather | solution.py:21
  156.3 33.6 %gather_fusion.1 = bf16[8192,256]{1,0:T(8,128)(2,1)} fusion(bf16[8192,256]{1,0:T(8,128)(2,1)} %all-gather.3.cloned.1.call-done, s32[8192]{0:T(1024)S(1)} %broadcast_clamp_fusion), kind=kCustom, calls=%fused_computation.1 | custom fusion | bytes 8421376 | tf_op jit(solution)/shard_map/jit(_take)/gather | solution.py:12
  189.9 5.6 %fusion.2 = f32[512,1,16]{2,1,0:T(1,128)S(1)} fusion(bf16[512,16,256]{2,1,0:T(8,128)(2,1)} %bitcast.16, pred[512,16]{1,0:T(8,128)(4,1)S(1)} %copy.12, bf16[512,256,1]{1,0,2:T(8,128)(2,1)S(1)} %bitcast.17), kind=kOutput, calls=%fused_computation.6 | convolution fusion | flops 6291456 | bytes 4497408 | tf_op jit(solution)/shard_map/rd,rkd->rk/dot_general | solution.py:13
  195.6 0.1 copy.14
  195.7 3.4 multiply_reduce_fusion
  199.0 45.5 %gather_fusion = f32[8192]{0:T(1024)S(1)} fusion(f32[8192]{0:T(1024)S(1)} %multiply_reduce_fusion, s32[8192]{0:T(1024)S(1)} %broadcast_clamp_fusion), kind=kCustom, calls=%fused_computation | custom fusion | bytes 98304 | tf_op jit(solution)/shard_map/jit(_take)/gather | solution.py:15
  244.6 0.1 reshape.19
  244.7 0.1 copy.11
  244.8 9.9 %fusion.12 = (f32[512]{0:T(512)S(1)}, bf16[512,8192]{1,0:T(8,128)(2,1)}) fusion(f32[512]{0:T(512)S(1)} %multiply_add_fusion, bf16[512,256]{1,0:T(8,128)(2,1)S(1)} %all_gather.9, bf16[8192,256]{1,0:T(8,128)(2,1)} %all-gather.3.cloned.1.call-done, f32[8192]{0:T(1024)S(1)} %multiply_reduce_fusion, f32[512]{0:T(512)S(1)} %multiply_reduce_fusion.1), kind=kOutput, calls=%fused_computation.21 | convolution fusion | flops 2176843264 | bytes 12883968 | tf_op jit(solution)/shard_map/dot_general | solution.py:29
  254.8 145.1 %all-to-all-done = bf16[32,256,1024]{2,1,0:T(8,128)(2,1)} async-done(((bf16[32,256,1024]{2,1,0:T(8,128)(2,1)}), bf16[32,256,1024]{2,1,0:T(8,128)(2,1)}, u32[]{:S(2)}, u32[]{:S(2)}) %all-to-all-start) | async-done | bytes 16777248 | tf_op jit(solution)/shard_map/all_to_all | solution.py:37
  399.9 15.6 %divide_convert_fusion = bf16[512,1024]{1,0:T(8,128)(2,1)} fusion(bf16[8192,1024]{1,0:T(8,128)(2,1)} %bitcast.4, bf16[512,8192]{1,0:T(8,128)(2,1)} %get-tuple-element.6, f32[512]{0:T(512)S(1)} %get-tuple-element.5), kind=kOutput, calls=%fused_computation.9 | convolution fusion | flops 8590983168 | bytes 26216448 | tf_op jit(solution)/shard_map/dot_general | solution.py:34
  (6 shorter events, 0.1 us)
Async XLA Ops:
  13.3 13.7 %copy-start.1 = (s32[64,16]{0,1:T(8,128)S(1)}, s32[64,16]{0,1:T(8,128)}, u32[]{:S(2)}) copy-start(s32[64,16]{0,1:T(8,128)} %param.6) | copy-start | bytes 12292
  13.3 38.7 %copy-start = (bf16[64,256]{1,0:T(8,128)(2,1)S(1)}, bf16[64,256]{1,0:T(8,128)(2,1)}, u32[]{:S(2)}) copy-start(bf16[64,256]{1,0:T(8,128)(2,1)} %param.4) | copy-start | bytes 98308
  13.3 386.5 %all-to-all-start = ((bf16[32,256,1024]{2,1,0:T(8,128)(2,1)}), bf16[32,256,1024]{2,1,0:T(8,128)(2,1)}, u32[]{:S(2)}, u32[]{:S(2)}) async-start(bf16[32,256,1024]{2,1,0:T(8,128)(2,1)} %stack.2), calls=%async_computation | async-start | bytes 33554432 | tf_op jit(solution)/shard_map/all_to_all | solution.py:37
  26.3 130.0 %all-gather.3.cloned.1.call-start = ((), (), s32[]{:S(2)}) async-start(), calls=%async_computation.1 | async-start | bytes 4325376 | tf_op jit(solution)/shard_map/all_gather | solution.py:21
Sparse Core Ops, SparseCore 0:
  29.9 126.3 all-gather.2
